TPU v7x, 512 devices: a whole 4x4x16 slice. The times are simulated.
512 devices in a mesh: row: 32 (over x, y, core), col: 16 (over z).
Axes of the slice: x: 4, y: 4, z: 16, core: 2. Of those that a mesh axis runs over, the one named last changes fastest.
Arguments:
- features: bfloat16 [65536, 256], P('col', 'row'), may hold values from -6 to 6
- weight: bfloat16 [256, 256], replicated, may hold values from -0.375 to 0.375
- adj_values: bfloat16 [32, 16, 96, 128, 128], P('row', 'col'), may hold values from -0.0625 to 0.0625
- block_rows: int32 [32, 16, 96], P('row', 'col'), may hold values from 0 to 15, as said below
- block_cols: int32 [32, 16, 96], P('row', 'col'), may hold values from 0 to 31
- block_counts: int32 [32, 16], P('row', 'col'), may hold values from 1 to 96, as said below
- cotangent: bfloat16 [65536, 256], P(('row', 'col')), may hold values from -6 to 6
Outputs:
- output: bfloat16 [65536, 256], P(('row', 'col'))
- grad_weight: float32 [256, 256], replicated
- grad_features: bfloat16 [65536, 256], P('col', 'row')
Inputs may be any that keep to these rules, and one draw needn't show every extreme that they name: Within one tile the pairs (block_rows, block_cols) over all 96 slots are distinct. `block_counts`: some tile holds exactly 96 live blocks and some other tile exactly one in every draw.
All inputs are finite; a program needn't handle non-finite values.
Results may differ from a plain program's by a relative error of at most 0.029.
Values may be sent and summed in bfloat16 or wider, within the bound.
A program may use at most 64 MiB of HBM per device.

v0:
```python
import math
import jax
import jax.numpy as jnp
from jax import lax
from jax.sharding import PartitionSpec as P

RB = 16


def block_product(tile_values, tile_rows, tile_cols, live_count, panels, out_blocks, transposed):
    padded = tile_values.shape[0]
    blocks_turn = math.gcd(padded, 16)
    block_size = panels.shape[1]
    columns = panels.shape[2]
    turns_needed = (live_count + blocks_turn - 1) // blocks_turn

    def step(turn_index, running):
        offset = turn_index * blocks_turn
        values_now = lax.dynamic_slice_in_dim(tile_values, offset, blocks_turn, 0)
        row_ids = lax.dynamic_slice_in_dim(tile_rows, offset, blocks_turn, 0)
        col_ids = lax.dynamic_slice_in_dim(tile_cols, offset, blocks_turn, 0)
        is_live = offset + jnp.arange(blocks_turn, dtype=jnp.int32) < live_count
        if transposed:
            picked = jnp.take(panels, row_ids, axis=0)
            product = jnp.einsum(
                "bij,bif->bjf", values_now, picked, preferred_element_type=jnp.float32
            )
            target_ids = col_ids
        else:
            picked = jnp.take(panels, col_ids, axis=0)
            product = jnp.einsum(
                "bij,bjf->bif", values_now, picked, preferred_element_type=jnp.float32
            )
            target_ids = row_ids
        contribution = jnp.where(is_live[:, None, None], product, 0.0)
        return running.at[target_ids].add(contribution)

    start_sum = jnp.zeros((out_blocks, block_size, columns), jnp.float32)
    return lax.fori_loop(0, turns_needed, step, start_sum)


def shards(features, weight, adj_values, block_rows, block_cols, block_counts, cotangent):
    tile_values = adj_values[0, 0]
    tile_rows = block_rows[0, 0]
    tile_cols = block_cols[0, 0]
    live_count = block_counts[0, 0]
    block_size = tile_values.shape[1]
    col_blocks = features.shape[0] // block_size
    node_total = col_blocks * block_size * lax.axis_size("col")
    panel_part = lax.all_gather(features, "row", axis=1, tiled=True)
    panels = panel_part.reshape(col_blocks, block_size, panel_part.shape[1])
    partial_value = block_product(tile_values, tile_rows, tile_cols, live_count, panels, RB, False)
    partial_value = partial_value.reshape(RB * block_size, partial_value.shape[2])
    aggregated = lax.psum_scatter(
        partial_value.astype(jnp.bfloat16), "col", scatter_dimension=0, tiled=True
    )
    preact = jnp.dot(aggregated, weight, preferred_element_type=jnp.float32)
    output = jax.nn.silu(preact).astype(jnp.bfloat16)
    sigmoid_pre = jax.nn.sigmoid(preact)
    slopes = sigmoid_pre * (1.0 + preact * (1.0 - sigmoid_pre))
    deltas = (cotangent.astype(jnp.float32) * slopes).astype(jnp.bfloat16)
    local_grad = jnp.dot(aggregated.T, deltas, preferred_element_type=jnp.float32)
    grad_weight = lax.psum(local_grad, ("row", "col")) * (1.0 / math.sqrt(node_total))
    backward = jnp.dot(deltas, weight.T, preferred_element_type=jnp.float32).astype(jnp.bfloat16)
    back_slab = lax.all_gather(backward, "col", axis=0, tiled=True)
    back_panels = back_slab.reshape(RB, block_size, back_slab.shape[1])
    column_terms = block_product(
        tile_values, tile_rows, tile_cols, live_count, back_panels, col_blocks, True
    )
    column_terms = column_terms.reshape(col_blocks * block_size, column_terms.shape[2])
    grad_features = lax.psum_scatter(
        column_terms.astype(jnp.bfloat16), "row", scatter_dimension=1, tiled=True
    )
    return (output, grad_weight, grad_features)


def solution(mesh):
    return jax.shard_map(
        shards,
        mesh=mesh,
        in_specs=(
            P("col", "row"),
            P(),
            P("row", "col", None, None, None),
            P("row", "col", None),
            P("row", "col", None),
            P("row", "col"),
            P(("row", "col"), None),
        ),
        out_specs=(P(("row", "col"), None), P(), P("col", "row")),
        check_vma=False,
    )
```

profile of v0, /device:TPU:2, one launch (start us, length us, event | category | flops | bytes accessed | tf_op | source)
XLA Modules:
  0.0 847.8 jit_solution(3140927563884392423)
XLA Ops:
  8.6 65.7 %all-gather.3.cloned.1.call-done = bf16[4096,256]{0,1:T(8,128)(2,1)} async-done(((bf16[4096,8]{0,1:T(8,128)(2,1)}), bf16[4096,256]{0,1:T(8,128)(2,1)}) %all-gather.3.cloned.1.call-update) | async-done | bytes 2097168 | tf_op jit(solution)/shard_map/all_gather | solution.py:50
  74.3 4.1 copy.11
  78.4 1.5 broadcast_in_dim.58
  80.0 35.9 %while.20 = (s32[]{:T(128)}, f32[16,128,256]{2,1,0:T(8,128)}, s32[]{:T(128)}, s32[96]{0:T(128)S(1)}, s32[]{:T(128)}, /*index=5*/bf16[96,128,128]{2,1,0:T(8,128)(...) while((s32[]{:T(128)}, f32[16,128,256]{2,1,0:T(8,128)}, ...), condition=%wide.region_2.3_spmd, body=%wide.region_0.2_spmd.sunk | while | flops 135791792 | bytes 12063415 | solution.py:39
  80.0 0.7 compare_and_fusion.4
  80.7 2.2 gather_fusion
  82.9 1.5 convolution_select_fusion.4
  84.5 4.3 scatter_fusion
  88.9 0.7 compare_and_fusion.4
  89.6 2.2 gather_fusion
  91.8 1.6 convolution_select_fusion.4
  93.4 4.4 scatter_fusion
  97.8 0.7 compare_and_fusion.4
  98.5 2.2 gather_fusion
  100.8 1.5 convolution_select_fusion.4
  102.4 4.5 scatter_fusion
  106.8 0.7 compare_and_fusion.4
  107.6 2.2 gather_fusion
  109.8 1.6 convolution_select_fusion.4
  111.4 4.4 scatter_fusion
  115.9 2.8 convert_element_type.24
  118.8 87.5 %reduce-scatter.3.cloned.1.call-done = bf16[128,256]{1,0:T(8,128)(2,1)} async-done(((bf16[2048,256]{1,0:T(8,128)(2,1)}), bf16[128,256]{1,0:T(8,128)(2,1)}) %reduce-scatter.3.cloned.1.call-update) | async-done | bytes 65552 | tf_op jit(solution)/shard_map/reduce_scatter | solution.py:54
  206.3 1.7 multiply_convert_fusion
  208.0 0.8 convolution_convert_fusion
  208.9 2.8 copy.10
  211.7 0.9 fusion.12
  212.7 65.3 %all-gather.5.cloned.1.call-done = bf16[2048,256]{1,0:T(8,128)(2,1)} async-done(((bf16[128,256]{1,0:T(8,128)(2,1)}), bf16[2048,256]{1,0:T(8,128)(2,1)}) %all-gather.5.cloned.1.call-update) | async-done | bytes 1048592 | tf_op jit(solution)/shard_map/all_gather | solution.py:65
  278.1 2.4 broadcast_in_dim.59
  280.5 34.6 %while.21 = (s32[]{:T(128)}, f32[32,128,256]{2,1,0:T(8,128)}, s32[]{:T(128)}, s32[96]{0:T(128)S(1)}, s32[]{:T(128)}, /*index=5*/bf16[96,128,128]{1,2,0:T(8,128)(...) while((s32[]{:T(128)}, f32[32,128,256]{2,1,0:T(8,128)}, ...), condition=%wide.region_7.8_spmd, body=%wide.region_5.7_spmd.sunk | while | flops 135791792 | bytes 12063415 | solution.py:39
  281.2 1.8 gather_fusion.1
  283.1 1.6 convolution_select_fusion.5
  284.7 4.3 scatter_fusion.1
  289.8 1.8 gather_fusion.1
  291.6 1.5 convolution_select_fusion.5
  293.3 4.5 scatter_fusion.1
  297.7 0.7 compare_and_fusion.5
  298.5 1.8 gather_fusion.1
  300.3 1.6 convolution_select_fusion.5
  301.9 4.5 scatter_fusion.1
  306.4 0.7 compare_and_fusion.5
  307.1 1.8 gather_fusion.1
  309.0 1.6 convolution_select_fusion.5
  310.6 4.4 scatter_fusion.1
  315.1 2.5 convert_element_type.30
  317.6 2.9 copy.15
  320.5 418.5 %all-reduce.2.cloned.1.call-done = f32[256,256]{1,0:T(8,128)} async-done(((f32[256,256]{1,0:T(8,128)}), f32[256,256]{1,0:T(8,128)}) %all-reduce.2.cloned.1.call-update) | async-done | bytes 262160 | tf_op jit(solution)/shard_map/psum | solution.py:63
  739.0 1.7 broadcast_multiply_fusion
  740.6 100.6 %reduce-scatter.5.cloned.1.call-done = bf16[4096,8]{0,1:T(8,128)(2,1)} async-done(((bf16[4096,256]{0,1:T(8,128)(2,1)}), bf16[4096,8]{0,1:T(8,128)(2,1)}) %reduce-scatter.5.cloned.1.call-update) | async-done | bytes 65552 | tf_op jit(solution)/shard_map/reduce_scatter | solution.py:71
  (40 shorter events, 3.1 us)
Async XLA Ops:
  7.2 199.1 %copy-start = (bf16[256,256]{1,0:T(8,128)(2,1)S(1)}, bf16[256,256]{1,0:T(8,128)(2,1)}, u32[]{:S(2)}) copy-start(bf16[256,256]{1,0:T(8,128)(2,1)} %param.12) | copy-start | bytes 393220
  7.2 67.2 %all-gather.3.cloned.1.call-start = ((), (), s32[]{:S(2)}) async-start(), calls=%async_computation.2 | async-start | bytes 2162688 | tf_op jit(solution)/shard_map/all_gather | solution.py:50
  7.9 198.4 %reduce-scatter.3.cloned.1.call-start = ((), (), s32[]{:S(2)}) async-start(), calls=%async_computation.3 | async-start | bytes 1114112 | tf_op jit(solution)/shard_map/reduce_scatter | solution.py:54
  78.4 1.5 copy-start.3
  78.4 1.5 copy-start.4
  115.9 90.4 %copy-start.5 = (bf16[128,256]{1,0:T(8,128)(2,1)S(1)}, bf16[128,256]{1,0:T(8,128)(2,1)}, u32[]{:S(2)}) copy-start(bf16[128,256]{1,0:T(8,128)(2,1)} %param.17) | copy-start | bytes 196612
  115.9 93.1 %copy-start.1 = (bf16[96,128,128]{2,1,0:T(8,128)(2,1)S(1)}, bf16[96,128,128]{2,1,0:T(8,128)(2,1)}, u32[]{:S(2)}) copy-start(bf16[96,128,128]{2,1,0:T(8,128)(2,1)} %get-tuple-element.328) | copy-start | bytes 9437188
  118.7 159.3 %all-gather.5.cloned.1.call-start = ((), (), s32[]{:S(2)}) async-start(), calls=%async_computation.5 | async-start | bytes 1114112 | tf_op jit(solution)/shard_map/all_gather | solution.py:65
  208.9 2.9 copy-start.2
  208.9 530.1 %all-reduce.2.cloned.1.call-start = ((), (), s32[]{:S(2)}) async-start(), calls=%async_computation.4 | async-start | bytes 524288 | tf_op jit(solution)/shard_map/psum | solution.py:63
  212.7 628.6 %reduce-scatter.5.cloned.1.call-start = ((), (), s32[]{:S(2)}) async-start(), calls=%async_computation.6 | async-start | bytes 2162688 | tf_op jit(solution)/shard_map/reduce_scatter | solution.py:71
Sparse Core Ops, SparseCore 0:
  11.1 63.1 all-gather.2
  118.9 87.4 reduce-scatter.2
  209.2 68.8 all-gather.4
  284.8 454.1 all-reduce.1
  743.8 97.3 reduce-scatter.4
where the time goes:
time: 850 us; the launch traced here: 848 us
  waiting for transfers between devices  738 us (87%)
  other arithmetic  48.7 us (6%)
  local copies, waits for them, and re-layouts  30 us (4%)
  matrix products  15.8 us (2%)
  between operations  14.5 us (2%)
    psum x1, waiting for transfers between devices, shards(): lax.psum(local_grad, ('row', 'col')) * (1.0 / math.sqrt(node_total))  418 us
    reduce_scatter x1, waiting for transfers between devices, shards(): lax.psum_scatter(column_terms.astype(jnp.bfloat16), 'row', scatter_dimens...  101 us
    reduce_scatter x1, waiting for transfers between devices, shards(): lax.psum_scatter(partial_value.astype(jnp.bfloat16), 'col', scatter_dimen...  87.5 us
    all_gather x1, waiting for transfers between devices, shards(): panel_part = lax.all_gather(features, 'row', axis=1, tiled=True)  65.7 us
    all_gather x1, waiting for transfers between devices, shards(): back_slab = lax.all_gather(backward, 'col', axis=0, tiled=True)  65.3 us
    scatter-add x8, other arithmetic, step(): return running.at[target_ids].add(contribution)  35.2 us
  transfers between devices with their start and end apart: 5, of which 5 were waited for; matrix products, arithmetic and copies ran while one was open for 6% of the time, Pallas kernels for 0%

commit v1 on v0

--- a/solution.py
+++ b/solution.py
@@ -60,7 +60,7 @@
     slopes = sigmoid_pre * (1.0 + preact * (1.0 - sigmoid_pre))
     deltas = (cotangent.astype(jnp.float32) * slopes).astype(jnp.bfloat16)
     local_grad = jnp.dot(aggregated.T, deltas, preferred_element_type=jnp.float32)
-    grad_weight = lax.psum(local_grad, ("row", "col")) * (1.0 / math.sqrt(node_total))
+    grad_weight = lax.psum(lax.psum(local_grad, "row"), "col") * (1.0 / math.sqrt(node_total))
     backward = jnp.dot(deltas, weight.T, preferred_element_type=jnp.float32).astype(jnp.bfloat16)
     back_slab = lax.all_gather(backward, "col", axis=0, tiled=True)
     back_panels = back_slab.reshape(RB, block_size, back_slab.shape[1])

time: 850 us -> 661 us (0.78)
  waiting for transfers between devices: 738 us -> 548 us
    psum x1 -> x2, waiting for transfers between devices: 418 us -> 218 us  [the longest x1 126 us: shards(): lax.psum(local_grad, 'row')]
  transfers between devices with their start and end apart: 5 -> 6, of which waited for: 5 -> 6; matrix products, arithmetic and copies ran while one was open for 6% -> 7% of each run, Pallas kernels for 0% -> 0%
where the time goes in v1:
time: 661 us; the launch traced here: 659 us
  waiting for transfers between devices  548 us (83%)
  other arithmetic  48.9 us (7%)
  local copies, waits for them, and re-layouts  30 us (5%)
  matrix products  16.7 us (3%)
  between operations  14.8 us (2%)
    psum x1, waiting for transfers between devices, shards(): lax.psum(local_grad, 'row')  126 us
    reduce_scatter x1, waiting for transfers between devices, shards(): lax.psum_scatter(column_terms.astype(jnp.bfloat16), 'row', scatter_dimens...  102 us
    psum x1, waiting for transfers between devices, shards(): lax.psum(lax.psum(local_grad, 'row'), 'col') * (1.0 / math.sqrt(node_total))  92 us
    reduce_scatter x1, waiting for transfers between devices, shards(): lax.psum_scatter(partial_value.astype(jnp.bfloat16), 'col', scatter_dimen...  87.6 us
    all_gather x1, waiting for transfers between devices, shards(): back_slab = lax.all_gather(backward, 'col', axis=0, tiled=True)  73.8 us
    all_gather x1, waiting for transfers between devices, shards(): panel_part = lax.all_gather(features, 'row', axis=1, tiled=True)  65.7 us
    scatter-add x8, other arithmetic, step(): return running.at[target_ids].add(contribution)  35.4 us
  transfers between devices with their start and end apart: 6, of which 6 were waited for; matrix products, arithmetic and copies ran while one was open for 7% of the time, Pallas kernels for 0%

profile of v1, /device:TPU:2, one launch (start us, length us, event | category | flops | bytes accessed | tf_op | source)
XLA Modules:
  0.0 659.2 jit_solution(12902511653311203061)
XLA Ops:
  8.6 65.7 %all-gather.3.cloned.1.call-done = bf16[4096,256]{0,1:T(8,128)(2,1)} async-done(((bf16[4096,8]{0,1:T(8,128)(2,1)}), bf16[4096,256]{0,1:T(8,128)(2,1)}) %all-gather.3.cloned.1.call-update) | async-done | bytes 2097168 | tf_op jit(solution)/shard_map/all_gather | solution.py:50
  74.3 4.1 copy.11
  78.4 1.5 broadcast_in_dim.58
  80.0 36.0 %while.20 = (s32[]{:T(128)}, f32[16,128,256]{2,1,0:T(8,128)}, s32[]{:T(128)}, s32[96]{0:T(128)S(1)}, s32[]{:T(128)}, /*index=5*/bf16[96,128,128]{2,1,0:T(8,128)(...) while((s32[]{:T(128)}, f32[16,128,256]{2,1,0:T(8,128)}, ...), condition=%wide.region_2.3_spmd, body=%wide.region_0.2_spmd.sunk | while | flops 135791792 | bytes 12063415 | solution.py:39
  80.0 0.7 compare_and_fusion.4
  80.7 2.2 gather_fusion
  82.9 1.6 convolution_select_fusion.4
  84.6 4.3 scatter_fusion
  88.9 0.7 compare_and_fusion.4
  89.6 2.2 gather_fusion
  91.8 1.6 convolution_select_fusion.4
  93.5 4.4 scatter_fusion
  97.9 0.7 compare_and_fusion.4
  98.6 2.2 gather_fusion
  100.8 1.5 convolution_select_fusion.4
  102.4 4.5 scatter_fusion
  106.9 0.7 compare_and_fusion.4
  107.6 2.2 gather_fusion
  109.8 1.6 convolution_select_fusion.4
  111.5 4.5 scatter_fusion
  115.9 2.8 convert_element_type.24
  118.9 87.6 %reduce-scatter.3.cloned.1.call-done = bf16[128,256]{1,0:T(8,128)(2,1)} async-done(((bf16[2048,256]{1,0:T(8,128)(2,1)}), bf16[128,256]{1,0:T(8,128)(2,1)}) %reduce-scatter.3.cloned.1.call-update) | async-done | bytes 65552 | tf_op jit(solution)/shard_map/reduce_scatter | solution.py:54
  206.5 1.7 multiply_convert_fusion
  208.2 1.8 fusion.12
  210.0 0.8 convolution_convert_fusion
  210.9 2.8 copy.10
  213.7 126.2 %all-reduce.3.cloned.1.call-done = f32[256,256]{1,0:T(8,128)} async-done(((f32[256,256]{1,0:T(8,128)}), f32[256,256]{1,0:T(8,128)}) %all-reduce.3.cloned.1.call-update) | async-done | bytes 262160 | tf_op jit(solution)/shard_map/psum | solution.py:63
  340.0 73.8 %all-gather.5.cloned.1.call-done = bf16[2048,256]{1,0:T(8,128)(2,1)} async-done(((bf16[128,256]{1,0:T(8,128)(2,1)}), bf16[2048,256]{1,0:T(8,128)(2,1)}) %all-gather.5.cloned.1.call-update) | async-done | bytes 1048592 | tf_op jit(solution)/shard_map/all_gather | solution.py:65
  413.8 2.4 broadcast_in_dim.59
  416.2 34.6 %while.21 = (s32[]{:T(128)}, f32[32,128,256]{2,1,0:T(8,128)}, s32[]{:T(128)}, s32[96]{0:T(128)S(1)}, s32[]{:T(128)}, /*index=5*/bf16[96,128,128]{1,2,0:T(8,128)(...) while((s32[]{:T(128)}, f32[32,128,256]{2,1,0:T(8,128)}, ...), condition=%wide.region_8.9_spmd, body=%wide.region_6.8_spmd.sunk | while | flops 135791792 | bytes 12063415 | solution.py:39
  416.2 0.7 compare_and_fusion.5
  417.0 1.8 gather_fusion.1
  418.8 1.6 convolution_select_fusion.5
  420.5 4.3 scatter_fusion.1
  425.5 1.8 gather_fusion.1
  427.4 1.6 convolution_select_fusion.5
  429.0 4.4 scatter_fusion.1
  434.2 1.8 gather_fusion.1
  436.0 1.6 convolution_select_fusion.5
  437.7 4.5 scatter_fusion.1
  442.9 1.8 gather_fusion.1
  444.8 1.6 convolution_select_fusion.5
  446.4 4.5 scatter_fusion.1
  450.9 2.5 convert_element_type.30
  453.4 3.0 copy.15
  456.3 92.0 %all-reduce.5.cloned.1.call-done = f32[256,256]{1,0:T(8,128)} async-done(((f32[256,256]{1,0:T(8,128)}), f32[256,256]{1,0:T(8,128)}) %all-reduce.5.cloned.1.call-update) | async-done | bytes 262160 | tf_op jit(solution)/shard_map/psum | solution.py:63
  548.4 1.7 broadcast_multiply_fusion
  550.1 102.3 %reduce-scatter.5.cloned.1.call-done = bf16[4096,8]{0,1:T(8,128)(2,1)} async-done(((bf16[4096,256]{0,1:T(8,128)(2,1)}), bf16[4096,8]{0,1:T(8,128)(2,1)}) %reduce-scatter.5.cloned.1.call-update) | async-done | bytes 65552 | tf_op jit(solution)/shard_map/reduce_scatter | solution.py:71
  (41 shorter events, 3.9 us)
Async XLA Ops:
  7.2 199.3 %copy-start = (bf16[256,256]{1,0:T(8,128)(2,1)S(1)}, bf16[256,256]{1,0:T(8,128)(2,1)}, u32[]{:S(2)}) copy-start(bf16[256,256]{1,0:T(8,128)(2,1)} %param.12) | copy-start | bytes 393220
  7.2 67.2 %all-gather.3.cloned.1.call-start = ((), (), s32[]{:S(2)}) async-start(), calls=%async_computation.2 | async-start | bytes 2162688 | tf_op jit(solution)/shard_map/all_gather | solution.py:50
  7.9 198.6 %reduce-scatter.3.cloned.1.call-start = ((), (), s32[]{:S(2)}) async-start(), calls=%async_computation.3 | async-start | bytes 1114112 | tf_op jit(solution)/shard_map/reduce_scatter | solution.py:54
  78.4 1.5 copy-start.2
  78.4 1.5 copy-start.3
  115.9 90.6 %copy-start.4 = (bf16[128,256]{1,0:T(8,128)(2,1)S(1)}, bf16[128,256]{1,0:T(8,128)(2,1)}, u32[]{:S(2)}) copy-start(bf16[128,256]{1,0:T(8,128)(2,1)} %param.17) | copy-start | bytes 196612
  115.9 95.0 %copy-start.1 = (bf16[96,128,128]{2,1,0:T(8,128)(2,1)S(1)}, bf16[96,128,128]{2,1,0:T(8,128)(2,1)}, u32[]{:S(2)}) copy-start(bf16[96,128,128]{2,1,0:T(8,128)(2,1)} %get-tuple-element.329) | copy-start | bytes 9437188
  118.8 221.1 %all-reduce.3.cloned.1.call-start = ((), (), s32[]{:S(2)}) async-start(), calls=%async_computation.4 | async-start | bytes 524288 | tf_op jit(solution)/shard_map/psum | solution.py:63
  210.0 203.8 %all-gather.5.cloned.1.call-start = ((), (), s32[]{:S(2)}) async-start(), calls=%async_computation.6 | async-start | bytes 1114112 | tf_op jit(solution)/shard_map/all_gather | solution.py:65
  210.9 337.5 %all-reduce.5.cloned.1.call-start = ((), (), s32[]{:S(2)}) async-start(), calls=%async_computation.5 | async-start | bytes 524288 | tf_op jit(solution)/shard_map/psum | solution.py:63
  339.9 312.5 %reduce-scatter.5.cloned.1.call-start = ((), (), s32[]{:S(2)}) async-start(), calls=%async_computation.7 | async-start | bytes 2162688 | tf_op jit(solution)/shard_map/reduce_scatter | solution.py:71
Sparse Core Ops, SparseCore 0:
  11.1 63.1 all-gather.2
  118.9 87.5 reduce-scatter.2
  210.6 129.2 all-reduce.2
  342.4 71.3 all-gather.4
  415.9 132.4 all-reduce.4
  553.9 98.4 reduce-scatter.4
